TPU v7x, 512 devices: a whole 4x4x16 slice. The times are simulated.
512 devices in a mesh: seq: 128 (over x, y, z_lo, core), head: 4 (over z_hi).
Axes of the slice: x: 4, y: 4, z: 16 (z_hi: 4, z_lo: 4; z = z_hi * 4 + z_lo), core: 2. Of those that a mesh axis runs over, the one named last changes fastest.
Arguments:
- queries: bfloat16 [16, 32768, 128], P('head', 'seq'), may hold values from -9 to 9
- key_vectors: bfloat16 [16, 32768, 128], P('head', 'seq'), may hold values from -9 to 9
- value_vectors: bfloat16 [16, 32768, 128], P('head', 'seq'), may hold values from -16 to 16
- block_perm: int32 [16, 64], P('head'), may hold values from 0 to 63, each once within a row
- out_weight: bfloat16 [16, 128, 2048], P('head'), may hold values from -0.125 to 0.125
- out_cotangent: bfloat16 [32768, 2048], P('seq', 'head'), may hold values from -6 to 6
Outputs:
- projected: bfloat16 [32768, 2048], P('seq', 'head')
- gradient_of_queries: bfloat16 [16, 32768, 128], P('head', 'seq')
- key_grad: bfloat16 [16, 32768, 128], P('head', 'seq')
- value_grad: bfloat16 [16, 32768, 128], P('head', 'seq')
Inputs may be any that keep to these rules, and one draw needn't show every extreme that they name: Each row of block_perm names every block of 0 to 63 once.
All inputs are finite; a program needn't handle non-finite values.
Results may differ from a plain program's by a relative error of at most 0.029.
Values may be sent and summed in bfloat16 or wider, within the bound.
A program may use at most 64 MiB of HBM per device.

v0:
```python
import math
import jax
import jax.numpy as jnp
from jax import lax
from jax.sharding import PartitionSpec as P


def partner(shard, axis, bit):
    return lax.ppermute(shard, axis, [(i, i ^ 1 << bit) for i in range(lax.axis_size(axis))])


def per_device(queries, key_vectors, value_vectors, block_perm, out_weight, out_cotangent):
    devices = lax.axis_size("seq")
    position = lax.axis_index("seq")
    parity = position % 2
    group_heads, tok_rows, head_width = queries.shape
    portion = tok_rows * head_width // devices
    score_scale = 1.0 / math.sqrt(head_width)
    owners = jnp.repeat(block_perm, 2, axis=1)
    indices = lax.iota(jnp.int32, devices)
    sources = [2 * owners, 2 * owners + 1]
    source_table = jnp.stack(sources, axis=1)
    slot_count = source_table.shape[1]
    select = (source_table[..., None] == indices).astype(jnp.bfloat16)
    stacked = jnp.stack([key_vectors, value_vectors])
    spread = lax.all_to_all(
        stacked.reshape(2, group_heads, devices, portion),
        "seq",
        split_axis=2,
        concat_axis=2,
        tiled=True,
    )
    picked = jnp.einsum(
        "hsij,chjl->chsil", select, spread, preferred_element_type=jnp.float32
    ).astype(jnp.bfloat16)
    routed = lax.all_to_all(picked, "seq", split_axis=3, concat_axis=3, tiled=True)
    routed = routed.reshape(2, group_heads, slot_count, tok_rows, head_width)
    partner_kv = routed.reshape(2, group_heads, 2 * tok_rows, head_width)
    pair_other = partner(stacked, "seq", 0)
    local_kv = jnp.where(
        parity == 0,
        jnp.concatenate([stacked, pair_other], 2),
        jnp.concatenate([pair_other, stacked], 2),
    )
    combined = jnp.concatenate([local_kv, partner_kv], 2)
    key_all = combined[0]
    value_all = combined[1]
    logit_scores = (
        jnp.einsum("htd,hkd->htk", queries, key_all, preferred_element_type=jnp.float32)
        * score_scale
    )
    row_max = jnp.max(logit_scores, axis=-1, keepdims=True)
    weights = jnp.exp(logit_scores - row_max)
    probabilities = weights / jnp.sum(weights, axis=-1, keepdims=True)
    reduced_probabilities = probabilities.astype(jnp.bfloat16)
    attention_result = jnp.einsum(
        "htk,hkd->htd", reduced_probabilities, value_all, preferred_element_type=jnp.float32
    ).astype(jnp.bfloat16)
    partial_out = jnp.einsum(
        "htd,hde->te", attention_result, out_weight, preferred_element_type=jnp.float32
    )
    summed = lax.psum(partial_out.astype(jnp.bfloat16), "head").astype(jnp.float32)
    columns = summed.shape[1] // lax.axis_size("head")
    result = lax.dynamic_slice_in_dim(summed, lax.axis_index("head") * columns, columns, 1)
    projected = result.astype(jnp.bfloat16)
    full_grad = lax.all_gather(out_cotangent, "head", axis=1, tiled=True)
    grad_att = jnp.einsum(
        "te,hde->htd", full_grad, out_weight, preferred_element_type=jnp.float32
    ).astype(jnp.bfloat16)
    row_delta = jnp.sum(
        grad_att.astype(jnp.float32) * attention_result.astype(jnp.float32), axis=-1, keepdims=True
    )
    probability_gradient = jnp.einsum(
        "htd,hkd->htk", grad_att, value_all, preferred_element_type=jnp.float32
    )
    score_gradient = (probabilities * (probability_gradient - row_delta) * score_scale).astype(
        jnp.bfloat16
    )
    gradient_of_queries = jnp.einsum(
        "htk,hkd->htd", score_gradient, key_all, preferred_element_type=jnp.float32
    ).astype(jnp.bfloat16)
    key_part = jnp.einsum(
        "htk,htd->hkd", score_gradient, queries, preferred_element_type=jnp.float32
    )
    value_part = jnp.einsum(
        "htk,htd->hkd", reduced_probabilities, grad_att, preferred_element_type=jnp.float32
    )
    gradients = jnp.stack([key_part, value_part])
    block_rows = 2 * tok_rows
    local_grad = gradients[:, :, :block_rows].reshape(2, group_heads, 2, tok_rows, head_width)
    own_grad = jnp.where(parity == 0, local_grad[:, :, 0], local_grad[:, :, 1])
    other_grad = jnp.where(parity == 0, local_grad[:, :, 1], local_grad[:, :, 0]).astype(
        jnp.bfloat16
    )
    partner_grad = gradients[:, :, block_rows:].reshape(2, group_heads, 2, tok_rows, head_width)
    partner_grad = partner_grad.astype(jnp.bfloat16)
    returned = lax.all_to_all(
        partner_grad.reshape(2, group_heads, slot_count, devices, portion),
        "seq",
        split_axis=3,
        concat_axis=3,
        tiled=True,
    )
    summed_back = jnp.einsum(
        "hsij,chsil->chjl", select, returned, preferred_element_type=jnp.float32
    ).astype(jnp.bfloat16)
    arrived = lax.all_to_all(summed_back, "seq", split_axis=2, concat_axis=2, tiled=True)
    arrived = arrived.reshape(2, group_heads, tok_rows, head_width).astype(jnp.float32)
    pair_back = partner(other_grad, "seq", 0).astype(jnp.float32)
    total_grad = own_grad + arrived + pair_back
    key_grad = total_grad[0].astype(jnp.bfloat16)
    value_grad = total_grad[1].astype(jnp.bfloat16)
    return (projected, gradient_of_queries, key_grad, value_grad)


def solution(mesh):
    return jax.shard_map(
        per_device,
        mesh=mesh,
        in_specs=(
            P("head", "seq", None),
            P("head", "seq", None),
            P("head", "seq", None),
            P("head", None),
            P("head", None, None),
            P("seq", "head"),
        ),
        out_specs=(
            P("seq", "head"),
            P("head", "seq", None),
            P("head", "seq", None),
            P("head", "seq", None),
        ),
        check_vma=False,
    )
```

profile of v0, /device:TPU:2, one launch (start us, length us, event | category | flops | bytes accessed | tf_op | source)
XLA Modules:
  0.0 314.9 jit_solution(3298835082028819904)
XLA Ops:
  7.2 1.2 stack.33
  8.4 1.0 stack.32
  9.5 1.3 copy.72
  10.8 13.0 %all-to-all-start = ((bf16[2,4,128,256]{3,0,1,2:T(2,128)(2,1)}), bf16[2,4,128,256]{3,0,1,2:T(2,128)(2,1)S(1)}, u32[]{:S(2)}, u32[]{:S(2)}) async-start(bf16[2,4,128,256]{3,0,1,2:T(2,128)(2,1)} %copy.72), calls=%async_computation | async-start | bytes 1048576 | tf_op jit(solution)/shard_map/all_to_all | solution.py:26
  24.1 16.4 %all-to-all-done = bf16[2,4,128,256]{3,0,1,2:T(2,128)(2,1)S(1)} async-done(((bf16[2,4,128,256]{3,0,1,2:T(2,128)(2,1)}), bf16[2,4,128,256]{3,0,1,2:T(2,128)(2,1)S(1)}, u32[]{:S(2)}, u32[]{:S(2)}) %all-to-all-start) | async-done | bytes 524320 | tf_op jit(solution)/shard_map/all_to_all | solution.py:26
  40.4 0.8 copy-done.14
  41.2 1.7 fusion.11
  42.9 2.1 copy.76
  45.0 9.3 %all-to-all-start.1 = ((bf16[2,4,2,128,256]{4,2,0,1,3:T(2,128)(2,1)}), bf16[2,4,2,128,256]{4,2,0,1,3:T(2,128)(2,1)}, u32[]{:S(2)}, u32[]{:S(2)}) async-start(bf16[2,4,2,128,256]{4,2,0,1,3:T(2,128)(2,1)} %copy.76), calls=%async_computation.1 | async-start | bytes 2097152 | tf_op jit(solution)/shard_map/all_to_all | solution.py:36
  54.5 2.2 collective-permute-start
  56.7 1.7 collective-permute-done
  58.4 1.6 maximum_select_fusion
  60.1 21.5 %all-to-all-done.1 = bf16[2,4,2,128,256]{4,2,0,1,3:T(2,128)(2,1)} async-done(((bf16[2,4,2,128,256]{4,2,0,1,3:T(2,128)(2,1)}), bf16[2,4,2,128,256]{4,2,0,1,3:T(2,128)(2,1)}, u32[]{:S(2)}, u32[]{:S(2)}) %all-to-all-start.1) | async-done | bytes 1048608 | tf_op jit(solution)/shard_map/all_to_all | solution.py:36
  81.6 2.5 copy.77
  84.1 2.3 reshape_reshape.3
  86.4 2.1 fusion.15
  88.5 4.6 %fusion.36 = (f32[4,256]{1,0:T(4,128)S(1)}, f32[4,256,1024]{1,2,0:T(8,128)}) fusion(bf16[4,1024,128]{2,1,0:T(8,128)(2,1)} %fusion.15, bf16[4,256,128]{2,1,0:T(8,128)(2,1)S(1)} %copy-done.15), kind=kOutput, calls=%fused_computation.63 | convolution fusion | flops 271582208 | bytes 5509120 | tf_op jit(solution)/shard_map/sub | solution.py:53
  93.1 2.6 fusion.10
  95.7 1.3 copy-done.3
  97.1 0.6 convolution_convert_fusion.3
  97.6 16.3 %all-gather.2.cloned.1.call-done = bf16[256,2048]{1,0:T(8,128)(2,1)} async-done(((bf16[256,512]{1,0:T(8,128)(2,1)}), bf16[256,2048]{1,0:T(8,128)(2,1)}) %all-gather.2.cloned.1.call-update) | async-done | bytes 1048592 | tf_op jit(solution)/shard_map/all_gather | solution.py:66
  113.9 2.1 fusion.22
  116.1 0.7 convolution_bitcast_fusion.1
  116.8 0.3 copy-done.11
  117.1 0.5 copy-done.7
  117.5 0.8 multiply_convert_fusion
  118.5 0.7 convolution_bitcast_fusion.2
  119.2 0.6 copy-done.8
  119.8 1.3 copy-done.2
  121.1 0.2 fusion.8
  121.3 1.3 convert_element_type.88
  122.5 2.3 copy.86
  124.8 45.1 %all_to_all.20 = bf16[2,4,2,128,256]{4,2,0,1,3:T(2,128)(2,1)S(1)} all-to-all(bf16[2,4,2,128,256]{4,2,0,1,3:T(2,128)(2,1)S(1)} %copy.86), channel_id=1, replica_groups=mesh['seq'=128,'head'=4] {'seq'}, dimensions={3} | all-to-all | bytes 2097152 | tf_op jit(solution)/shard_map/all_to_all | solution.py:97
  169.9 0.9 fusion.13
  170.8 1.1 copy.88
  171.9 8.6 %all-to-all-start.3 = ((bf16[2,4,128,256]{3,0,1,2:T(2,128)(2,1)}), bf16[2,4,128,256]{3,0,1,2:T(2,128)(2,1)S(1)}, u32[]{:S(2)}, u32[]{:S(2)}) async-start(bf16[2,4,128,256]{3,0,1,2:T(2,128)(2,1)} %copy.88), calls=%async_computation.3 | async-start | bytes 1048576 | tf_op jit(solution)/shard_map/all_to_all | solution.py:107
  180.6 1.8 fusion.6
  182.4 1.8 fusion.7
  184.3 1.3 copy-done.5
  185.5 0.9 fusion.21
  186.4 2.0 collective-permute-start.1
  188.5 1.6 convolution_convert_fusion.1
  190.1 111.2 %all-reduce.2.cloned.1.call-done = bf16[256,2048]{1,0:T(8,128)(2,1)} async-done(((bf16[256,2048]{1,0:T(8,128)(2,1)}), bf16[256,2048]{1,0:T(8,128)(2,1)}) %all-reduce.2.cloned.1.call-update) | async-done | bytes 1048592 | tf_op jit(solution)/shard_map/psum | solution.py:62
  301.3 1.7 convert_convert_fusion
  302.9 1.1 copy_convert_fusion
  304.0 1.3 reshape.55
  305.3 1.9 fusion.18
  307.3 0.8 slice_bitcast_fusion.2
  (43 shorter events, 0.6 us)
Async XLA Ops:
  7.2 106.8 %copy-start = (bf16[4,128,2048]{2,1,0:T(8,128)(2,1)S(1)}, bf16[4,128,2048]{2,1,0:T(8,128)(2,1)}, u32[]{:S(2)}) copy-start(bf16[4,128,2048]{2,1,0:T(8,128)(2,1)} %param.10) | copy-start | bytes 6291460
  7.2 16.6 %copy-start.17 = (s32[4,64]{1,0:T(4,128)S(1)}, s32[4,64]{1,0:T(4,128)}, u32[]{:S(2)}) copy-start(s32[4,64]{1,0:T(4,128)} %param.9) | copy-start | bytes 3076
  10.8 29.6 %all-to-all-start = ((bf16[2,4,128,256]{3,0,1,2:T(2,128)(2,1)}), bf16[2,4,128,256]{3,0,1,2:T(2,128)(2,1)S(1)}, u32[]{:S(2)}, u32[]{:S(2)}) async-start(bf16[2,4,128,256]{3,0,1,2:T(2,128)(2,1)} %copy.72), calls=%async_computation | async-start | bytes 1048576 | tf_op jit(solution)/shard_map/all_to_all | solution.py:26
  40.4 0.8 copy-start.14
  42.9 11.5 %copy-start.12 = (bf16[4,256,128]{2,1,0:T(8,128)(2,1)S(1)}, bf16[4,256,128]{2,1,0:T(8,128)(2,1)}, u32[]{:S(2)}) copy-start(bf16[4,256,128]{2,1,0:T(8,128)(2,1)} %param.8) | copy-start | bytes 786436
  45.0 9.4 %copy-start.13 = (bf16[4,256,128]{2,1,0:T(8,128)(2,1)S(1)}, bf16[4,256,128]{2,1,0:T(8,128)(2,1)}, u32[]{:S(2)}) copy-start(bf16[4,256,128]{2,1,0:T(8,128)(2,1)} %param.7) | copy-start | bytes 786436
  45.0 36.6 %all-to-all-start.1 = ((bf16[2,4,2,128,256]{4,2,0,1,3:T(2,128)(2,1)}), bf16[2,4,2,128,256]{4,2,0,1,3:T(2,128)(2,1)}, u32[]{:S(2)}, u32[]{:S(2)}) async-start(bf16[2,4,2,128,256]{4,2,0,1,3:T(2,128)(2,1)} %copy.76), calls=%async_computation.1 | async-start | bytes 2097152 | tf_op jit(solution)/shard_map/all_to_all | solution.py:36
  54.3 59.6 %all-gather.2.cloned.1.call-start = ((), (), s32[]{:S(2)}) async-start(), calls=%async_computation.5 | async-start | bytes 1310720 | tf_op jit(solution)/shard_map/all_gather | solution.py:66
  54.5 3.9 %collective-permute-start = (bf16[2,4,256,128]{3,2,1,0:T(8,128)(2,1)S(1)}, bf16[2,4,256,128]{3,2,1,0:T(8,128)(2,1)}, u32[]{:S(2)}, u32[]{:S(2)}) collective-permute-start(bf16[2,4,256,128]{3,2,1,0:T(8,128)(2,1)S(1)} %pad_maximum_fusion.2), channel_id=1, source_target_pairs={{0,4},{4,0},{8,12},{12,8},{16,20},{20,16},{24,28},{28,24},{32,36},... | collective-permute-start | bytes 1572872 | tf_op jit(solution)/shard_map/ppermute | solution.py:9
  86.4 2.1 copy-start.15
  93.1 4.0 %copy-start.6 = (bf16[2,4,512,128]{3,2,1,0:T(8,128)(2,1)S(1)}, bf16[2,4,512,128]{3,2,1,0:T(8,128)(2,1)}, u32[]{:S(2)}) copy-start(bf16[2,4,512,128]{3,2,1,0:T(8,128)(2,1)} %reshape_reshape.3) | copy-start | bytes 3145732
  95.7 1.3 copy-start.3
  113.9 2.1 copy-start.4
  113.9 3.1 copy-start.11
  116.1 1.5 copy-start.7
  116.8 2.4 copy-start.1
  117.5 0.9 copy-start.16
  118.5 1.3 copy-start.8
  119.8 1.3 copy-start.2
  171.9 131.0 %all-to-all-start.3 = ((bf16[2,4,128,256]{3,0,1,2:T(2,128)(2,1)}), bf16[2,4,128,256]{3,0,1,2:T(2,128)(2,1)S(1)}, u32[]{:S(2)}, u32[]{:S(2)}) async-start(bf16[2,4,128,256]{3,0,1,2:T(2,128)(2,1)} %copy.88), calls=%async_computation.3 | async-start | bytes 1048576 | tf_op jit(solution)/shard_map/all_to_all | solution.py:107
  180.5 120.8 %all-reduce.2.cloned.1.call-start = ((), (), s32[]{:S(2)}) async-start(), calls=%async_computation.4 | async-start | bytes 2097152 | tf_op jit(solution)/shard_map/psum | solution.py:62
  182.4 6.1 %copy-start.9 = (bf16[4,256,1024]{1,2,0:T(8,128)(2,1)S(1)}, bf16[4,256,1024]{1,2,0:T(8,128)(2,1)}, u32[]{:S(2)}) copy-start(bf16[4,256,1024]{1,2,0:T(8,128)(2,1)} %copy-done.8) | copy-start | bytes 6291460
  182.4 6.1 %copy-start.10 = (bf16[4,1024,128]{2,1,0:T(8,128)(2,1)S(1)}, bf16[4,1024,128]{2,1,0:T(8,128)(2,1)}, u32[]{:S(2)}) copy-start(bf16[4,1024,128]{2,1,0:T(8,128)(2,1)} %fusion.15) | copy-start | bytes 3145732
  184.2 1.3 copy-start.5
  186.4 118.9 %collective-permute-start.1 = (bf16[2,4,256,128]{3,2,1,0:T(8,128)(2,1)}, bf16[2,4,256,128]{3,2,1,0:T(8,128)(2,1)}, u32[]{:S(2)}, u32[]{:S(2)}) collective-permute-start(bf16[2,4,256,128]{3,2,1,0:T(8,128)(2,1)} %fusion.21), channel_id=1, source_target_pairs={{0,4},{4,0},{8,12},{12,8},{16,20},{20,16},{24,28},{28,24},{32,36},... | collective-permute-start | bytes 1572872 | tf_op jit(solution)/shard_map/ppermute | solution.py:9
Sparse Core Ops, SparseCore 0:
  57.3 56.6 all-gather.1
  184.3 116.9 all-reduce.1
where the time goes:
time: 316 us; the launch traced here: 315 us
  waiting for transfers between devices  167 us (53%)
  blocking collectives  45.1 us (14%)
  starting transfers between devices  35.3 us (11%)
  local copies, waits for them, and re-layouts  23.7 us (8%)
  matrix products  15.4 us (5%)
  between operations  14.4 us (5%)
  other arithmetic  14.1 us (4%)
    psum x1, waiting for transfers between devices, per_device(): lax.psum(partial_out.astype(jnp.bfloat16), 'head').astype(jnp.float32)  111 us
    all_to_all x1, blocking collectives, per_device(): lax.all_to_all(partner_grad.reshape(2, group_heads, slot_count, devices,...  45.1 us
    all_to_all x1, waiting for transfers between devices, per_device(): lax.all_to_all(picked, 'seq', split_axis=3, concat_axis=3, tiled=True)  21.5 us
    all_to_all x1, waiting for transfers between devices, per_device(): lax.all_to_all(stacked.reshape(2, group_heads, devices, portion), 'seq',...  16.4 us
    all_gather x1, waiting for transfers between devices, per_device(): full_grad = lax.all_gather(out_cotangent, 'head', axis=1, tiled=True)  16.3 us
    all_to_all x1, starting transfers between devices, per_device(): lax.all_to_all(stacked.reshape(2, group_heads, devices, portion), 'seq',...  13 us
    all_to_all x1, starting transfers between devices, per_device(): lax.all_to_all(picked, 'seq', split_axis=3, concat_axis=3, tiled=True)  9.32 us
    all_to_all x1, starting transfers between devices, per_device(): lax.all_to_all(summed_back, 'seq', split_axis=2, concat_axis=2, tiled=True)  8.6 us
  transfers between devices with their start and end apart: 7, of which 5 were waited for; matrix products, arithmetic and copies ran while one was open for 8% of the time, Pallas kernels for 0%

commit v1 on v0

--- a/solution.py
+++ b/solution.py
@@ -3,6 +3,11 @@
 import jax.numpy as jnp
 from jax import lax
 from jax.sharding import PartitionSpec as P
+
+
+def gather_and_add(block, axis):
+    parts = lax.all_gather(block, axis)
+    return jnp.sum(parts, axis=0)
 
 
 def partner(shard, axis, bit):
@@ -59,7 +64,7 @@
     partial_out = jnp.einsum(
         "htd,hde->te", attention_result, out_weight, preferred_element_type=jnp.float32
     )
-    summed = lax.psum(partial_out.astype(jnp.bfloat16), "head").astype(jnp.float32)
+    summed = gather_and_add(partial_out.astype(jnp.bfloat16), "head").astype(jnp.float32)
     columns = summed.shape[1] // lax.axis_size("head")
     result = lax.dynamic_slice_in_dim(summed, lax.axis_index("head") * columns, columns, 1)
     projected = result.astype(jnp.bfloat16)

time: 316 us -> 341 us (1.079)
  the two profiles are of different devices: /device:TPU:2 before, /device:TPU:1 now
where the time goes in v1:
time: 341 us; the launch traced here: 340 us
  waiting for transfers between devices  142 us (42%)
  starting transfers between devices  125 us (37%)
  local copies, waits for them, and re-layouts  25.9 us (8%)
  other arithmetic  16.3 us (5%)
  matrix products  16.1 us (5%)
  between operations  14.4 us (4%)
    all_to_all x1, starting transfers between devices, per_device(): lax.all_to_all(summed_back, 'seq', split_axis=2, concat_axis=2, tiled=True)  82 us
    all_to_all x1, waiting for transfers between devices, per_device(): lax.all_to_all(summed_back, 'seq', split_axis=2, concat_axis=2, tiled=True)  51.2 us
    all_to_all x1, waiting for transfers between devices, per_device(): lax.all_to_all(partner_grad.reshape(2, group_heads, slot_count, devices,...  32.5 us
    all_to_all x1, waiting for transfers between devices, per_device(): lax.all_to_all(picked, 'seq', split_axis=3, concat_axis=3, tiled=True)  22.8 us
    all_to_all x1, waiting for transfers between devices, per_device(): lax.all_to_all(stacked.reshape(2, group_heads, devices, portion), 'seq',...  18 us
    all_gather x1, waiting for transfers between devices, per_device(): full_grad = lax.all_gather(out_cotangent, 'head', axis=1, tiled=True)  16.3 us
    all_to_all x1, starting transfers between devices, per_device(): lax.all_to_all(partner_grad.reshape(2, group_heads, slot_count, devices,...  15.9 us
    all_to_all x1, starting transfers between devices, per_device(): lax.all_to_all(stacked.reshape(2, group_heads, devices, portion), 'seq',...  13.8 us
  transfers between devices with their start and end apart: 8, of which 6 were waited for; matrix products, arithmetic and copies ran while one was open for 9% of the time, Pallas kernels for 0%

profile of v1, /device:TPU:1, one launch (start us, length us, event | category | flops | bytes accessed | tf_op | source)
XLA Modules:
  0.0 340.4 jit_solution(4021444114260147889)
XLA Ops:
  7.2 1.2 stack.32
  8.4 1.0 stack.33
  9.5 1.3 copy.72
  10.8 13.8 %all-to-all-start = ((bf16[2,4,128,256]{3,0,1,2:T(2,128)(2,1)}), bf16[2,4,128,256]{3,0,1,2:T(2,128)(2,1)S(1)}, u32[]{:S(2)}, u32[]{:S(2)}) async-start(bf16[2,4,128,256]{3,0,1,2:T(2,128)(2,1)} %copy.72), calls=%async_computation | async-start | bytes 1048576 | tf_op jit(solution)/shard_map/all_to_all | solution.py:31
  24.9 18.0 %all-to-all-done = bf16[2,4,128,256]{3,0,1,2:T(2,128)(2,1)S(1)} async-done(((bf16[2,4,128,256]{3,0,1,2:T(2,128)(2,1)}), bf16[2,4,128,256]{3,0,1,2:T(2,128)(2,1)S(1)}, u32[]{:S(2)}, u32[]{:S(2)}) %all-to-all-start) | async-done | bytes 524320 | tf_op jit(solution)/shard_map/all_to_all | solution.py:31
  43.0 0.8 copy-done.14
  43.8 1.7 fusion.11
  45.5 2.1 copy.76
  47.5 7.5 %all-to-all-start.1 = ((bf16[2,4,2,128,256]{4,2,0,1,3:T(2,128)(2,1)}), bf16[2,4,2,128,256]{4,2,0,1,3:T(2,128)(2,1)}, u32[]{:S(2)}, u32[]{:S(2)}) async-start(bf16[2,4,2,128,256]{4,2,0,1,3:T(2,128)(2,1)} %copy.76), calls=%async_computation.1 | async-start | bytes 2097152 | tf_op jit(solution)/shard_map/all_to_all | solution.py:41
  55.2 3.2 collective-permute-start
  58.4 1.4 collective-permute-done
  59.9 1.7 maximum_select_fusion
  61.6 22.8 %all-to-all-done.1 = bf16[2,4,2,128,256]{4,2,0,1,3:T(2,128)(2,1)} async-done(((bf16[2,4,2,128,256]{4,2,0,1,3:T(2,128)(2,1)}), bf16[2,4,2,128,256]{4,2,0,1,3:T(2,128)(2,1)}, u32[]{:S(2)}, u32[]{:S(2)}) %all-to-all-start.1) | async-done | bytes 1048608 | tf_op jit(solution)/shard_map/all_to_all | solution.py:41
  84.4 2.6 copy.77
  87.0 2.3 reshape_reshape.3
  89.3 2.1 fusion.15
  91.4 4.6 %fusion.36 = (f32[4,256]{1,0:T(4,128)S(1)}, f32[4,256,1024]{1,2,0:T(8,128)}) fusion(bf16[4,1024,128]{2,1,0:T(8,128)(2,1)} %fusion.15, bf16[4,256,128]{2,1,0:T(8,128)(2,1)S(1)} %copy-done.15), kind=kOutput, calls=%fused_computation.63 | convolution fusion | flops 271582208 | bytes 5509120 | tf_op jit(solution)/shard_map/sub | solution.py:58
  96.0 2.6 fusion.10
  98.7 1.3 copy-done.3
  100.0 0.6 convolution_convert_fusion.3
  100.6 16.3 %all-gather.4.cloned.1.call-done = bf16[256,2048]{1,0:T(8,128)(2,1)} async-done(((bf16[256,512]{1,0:T(8,128)(2,1)}), bf16[256,2048]{1,0:T(8,128)(2,1)}) %all-gather.4.cloned.1.call-update) | async-done | bytes 1048592 | tf_op jit(solution)/shard_map/all_gather | solution.py:71
  116.9 2.1 fusion.22
  119.1 0.7 convolution_bitcast_fusion.1
  120.1 0.5 copy-done.7
  120.5 0.8 multiply_convert_fusion
  121.5 0.7 convolution_bitcast_fusion.2
  122.2 0.6 copy-done.8
  122.8 1.4 copy-done.2
  124.4 1.2 convert_element_type.90
  125.6 3.3 copy.86
  128.9 15.9 %all-to-all-start.2 = ((bf16[2,4,2,128,256]{4,2,0,1,3:T(2,128)(2,1)}), bf16[2,4,2,128,256]{4,2,0,1,3:T(2,128)(2,1)S(1)}, u32[]{:S(2)}, u32[]{:S(2)}) async-start(bf16[2,4,2,128,256]{4,2,0,1,3:T(2,128)(2,1)} %copy.86), calls=%async_computation.2 | async-start | bytes 2097152 | tf_op jit(solution)/shard_map/all_to_all | solution.py:102
  144.9 1.7 fusion.6
  146.7 32.5 %all-to-all-done.2 = bf16[2,4,2,128,256]{4,2,0,1,3:T(2,128)(2,1)S(1)} async-done(((bf16[2,4,2,128,256]{4,2,0,1,3:T(2,128)(2,1)}), bf16[2,4,2,128,256]{4,2,0,1,3:T(2,128)(2,1)S(1)}, u32[]{:S(2)}, u32[]{:S(2)}) %all-to-all-start.2) | async-done | bytes 1048608 | tf_op jit(solution)/shard_map/all_to_all | solution.py:102
  179.2 1.6 fusion.13
  180.9 2.0 copy.88
  182.9 82.0 %all-to-all-start.3 = ((bf16[2,4,128,256]{3,0,1,2:T(2,128)(2,1)}), bf16[2,4,128,256]{3,0,1,2:T(2,128)(2,1)S(1)}, u32[]{:S(2)}, u32[]{:S(2)}) async-start(bf16[2,4,128,256]{3,0,1,2:T(2,128)(2,1)} %copy.88), calls=%async_computation.3 | async-start | bytes 1048576 | tf_op jit(solution)/shard_map/all_to_all | solution.py:112
  265.0 1.8 fusion.7
  266.8 1.4 copy-done.5
  268.2 0.9 fusion.21
  269.1 2.8 collective-permute-start.1
  271.9 1.6 convolution_convert_fusion.1
  273.5 51.2 %all-to-all-done.3 = bf16[2,4,128,256]{3,0,1,2:T(2,128)(2,1)S(1)} async-done(((bf16[2,4,128,256]{3,0,1,2:T(2,128)(2,1)}), bf16[2,4,128,256]{3,0,1,2:T(2,128)(2,1)S(1)}, u32[]{:S(2)}, u32[]{:S(2)}) %all-to-all-start.3) | async-done | bytes 524320 | tf_op jit(solution)/shard_map/all_to_all | solution.py:112
  324.6 1.1 copy_convert_fusion
  325.8 1.3 reshape.55
  327.1 1.9 fusion.18
  329.0 0.8 slice_bitcast_fusion.2
  329.8 3.1 reduce_sum.31
  332.9 0.7 convert_convert_fusion
  (45 shorter events, 1.1 us)
Async XLA Ops:
  7.2 109.8 %copy-start = (bf16[4,128,2048]{2,1,0:T(8,128)(2,1)S(1)}, bf16[4,128,2048]{2,1,0:T(8,128)(2,1)}, u32[]{:S(2)}) copy-start(bf16[4,128,2048]{2,1,0:T(8,128)(2,1)} %param.10) | copy-start | bytes 6291460
  7.2 17.5 %copy-start.17 = (s32[4,64]{1,0:T(4,128)S(1)}, s32[4,64]{1,0:T(4,128)}, u32[]{:S(2)}) copy-start(s32[4,64]{1,0:T(4,128)} %param.9) | copy-start | bytes 3076
  10.8 32.1 %all-to-all-start = ((bf16[2,4,128,256]{3,0,1,2:T(2,128)(2,1)}), bf16[2,4,128,256]{3,0,1,2:T(2,128)(2,1)S(1)}, u32[]{:S(2)}, u32[]{:S(2)}) async-start(bf16[2,4,128,256]{3,0,1,2:T(2,128)(2,1)} %copy.72), calls=%async_computation | async-start | bytes 1048576 | tf_op jit(solution)/shard_map/all_to_all | solution.py:31
  43.0 0.8 copy-start.14
  45.4 9.7 %copy-start.12 = (bf16[4,256,128]{2,1,0:T(8,128)(2,1)S(1)}, bf16[4,256,128]{2,1,0:T(8,128)(2,1)}, u32[]{:S(2)}) copy-start(bf16[4,256,128]{2,1,0:T(8,128)(2,1)} %param.8) | copy-start | bytes 786436
  47.5 7.6 %copy-start.13 = (bf16[4,256,128]{2,1,0:T(8,128)(2,1)S(1)}, bf16[4,256,128]{2,1,0:T(8,128)(2,1)}, u32[]{:S(2)}) copy-start(bf16[4,256,128]{2,1,0:T(8,128)(2,1)} %param.7) | copy-start | bytes 786436
  47.5 36.8 %all-to-all-start.1 = ((bf16[2,4,2,128,256]{4,2,0,1,3:T(2,128)(2,1)}), bf16[2,4,2,128,256]{4,2,0,1,3:T(2,128)(2,1)}, u32[]{:S(2)}, u32[]{:S(2)}) async-start(bf16[2,4,2,128,256]{4,2,0,1,3:T(2,128)(2,1)} %copy.76), calls=%async_computation.1 | async-start | bytes 2097152 | tf_op jit(solution)/shard_map/all_to_all | solution.py:41
  55.1 61.8 %all-gather.4.cloned.1.call-start = ((), (), s32[]{:S(2)}) async-start(), calls=%async_computation.4 | async-start | bytes 1310720 | tf_op jit(solution)/shard_map/all_gather | solution.py:71
  55.2 4.6 %collective-permute-start = (bf16[2,4,256,128]{3,2,1,0:T(8,128)(2,1)S(1)}, bf16[2,4,256,128]{3,2,1,0:T(8,128)(2,1)}, u32[]{:S(2)}, u32[]{:S(2)}) collective-permute-start(bf16[2,4,256,128]{3,2,1,0:T(8,128)(2,1)S(1)} %pad_maximum_fusion.2), channel_id=1, source_target_pairs={{0,4},{4,0},{8,12},{12,8},{16,20},{20,16},{24,28},{28,24},{32,36},... | collective-permute-start | bytes 1572872 | tf_op jit(solution)/shard_map/ppermute | solution.py:14
  89.3 2.2 copy-start.15
  96.0 4.0 %copy-start.6 = (bf16[2,4,512,128]{3,2,1,0:T(8,128)(2,1)S(1)}, bf16[2,4,512,128]{3,2,1,0:T(8,128)(2,1)}, u32[]{:S(2)}) copy-start(bf16[2,4,512,128]{3,2,1,0:T(8,128)(2,1)} %reshape_reshape.3) | copy-start | bytes 3145732
  98.7 1.3 copy-start.3
  116.9 2.1 copy-start.4
  116.9 3.1 copy-start.11
  119.1 1.5 copy-start.7
  119.8 2.4 copy-start.1
  120.5 0.9 copy-start.16
  121.5 1.3 copy-start.8
  122.8 1.4 copy-start.2
  128.9 50.3 %all-to-all-start.2 = ((bf16[2,4,2,128,256]{4,2,0,1,3:T(2,128)(2,1)}), bf16[2,4,2,128,256]{4,2,0,1,3:T(2,128)(2,1)S(1)}, u32[]{:S(2)}, u32[]{:S(2)}) async-start(bf16[2,4,2,128,256]{4,2,0,1,3:T(2,128)(2,1)} %copy.86), calls=%async_computation.2 | async-start | bytes 2097152 | tf_op jit(solution)/shard_map/all_to_all | solution.py:102
  144.9 184.9 %all-gather.6.cloned.1.call-start = ((), (), s32[]{:S(2)}) async-start(), calls=%async_computation.5 | async-start | bytes 5242880 | tf_op jit(solution)/shard_map/all_gather | solution.py:9
  182.9 141.8 %all-to-all-start.3 = ((bf16[2,4,128,256]{3,0,1,2:T(2,128)(2,1)}), bf16[2,4,128,256]{3,0,1,2:T(2,128)(2,1)S(1)}, u32[]{:S(2)}, u32[]{:S(2)}) async-start(bf16[2,4,128,256]{3,0,1,2:T(2,128)(2,1)} %copy.88), calls=%async_computation.3 | async-start | bytes 1048576 | tf_op jit(solution)/shard_map/all_to_all | solution.py:112
  264.9 7.0 %copy-start.9 = (bf16[4,256,1024]{1,2,0:T(8,128)(2,1)S(1)}, bf16[4,256,1024]{1,2,0:T(8,128)(2,1)}, u32[]{:S(2)}) copy-start(bf16[4,256,1024]{1,2,0:T(8,128)(2,1)} %copy-done.8) | copy-start | bytes 6291460
  264.9 7.0 %copy-start.10 = (bf16[4,1024,128]{2,1,0:T(8,128)(2,1)S(1)}, bf16[4,1024,128]{2,1,0:T(8,128)(2,1)}, u32[]{:S(2)}) copy-start(bf16[4,1024,128]{2,1,0:T(8,128)(2,1)} %fusion.15) | copy-start | bytes 3145732
  266.8 1.4 copy-start.5
  269.1 58.0 %collective-permute-start.1 = (bf16[2,4,256,128]{3,2,1,0:T(8,128)(2,1)}, bf16[2,4,256,128]{3,2,1,0:T(8,128)(2,1)}, u32[]{:S(2)}, u32[]{:S(2)}) collective-permute-start(bf16[2,4,256,128]{3,2,1,0:T(8,128)(2,1)} %fusion.21), channel_id=1, source_target_pairs={{0,4},{4,0},{8,12},{12,8},{16,20},{20,16},{24,28},{28,24},{32,36},... | collective-permute-start | bytes 1572872 | tf_op jit(solution)/shard_map/ppermute | solution.py:14
Sparse Core Ops, SparseCore 0:
  58.5 58.3 all-gather.3
  147.8 112.8 all-gather.5
